TPU v7x, 256 devices: a whole 4x4x8 slice. The times are simulated.
256 devices in a mesh: order: 64 (over z, x, core), lat: 4 (over y).
Axes of the slice: x: 4, y: 4, z: 8, core: 2. Of those that a mesh axis runs over, the one named last changes fastest.
Arguments:
- position: float32 [128, 2, 64, 2160], P('order', None, None, 'lat'), may hold values from -6 to 6
- residual: float32 [128, 2, 64, 2160], P('order', None, None, 'lat'), as said below
- direction: float32 [128, 2, 64, 2160], P('order', None, None, 'lat'), as said below
- legendre: float32 [128, 2160, 2048], P('order', None, 'lat'), may hold values from -0.125 to 0.125
- order_of: int32 [128], replicated, may hold values from 0 to 2032, as said below
- class_idx: int32 [2048, 4320], P(('lat', 'order')), may hold values from 0 to 15
- land: int32 [2048, 4320], P(('lat', 'order')), may hold values 0 or 1
- class_weight: float32 [16, 2], replicated, may hold values from 0.2 to 5
- damping: float32 [2160], P('lat'), may hold values from 0.05 to 0.5
Outputs:
- new_position: float32 [128, 2, 64, 2160], P('order', None, None, 'lat')
- new_residual: float32 [128, 2, 64, 2160], P('order', None, None, 'lat')
- new_direction: float32 [128, 2, 64, 2160], P('order', None, None, 'lat')
Inputs may be any that keep to these rules, and one draw needn't show every extreme that they name: `order_of`: distinct multiples of 16: each of 0, 16, ..., 16 * (128 - 1) appears exactly once. `residual`: real-valued and not zero. `direction`: real-valued and not zero.
All inputs are finite; a program needn't handle non-finite values. No bound on the sum of `land` on one device may be relied on, other than what follows from the above.
Results may differ from a plain program's by a relative error of at most 0.000058.
Values sent between devices are 32-bit elements; how exact they have to be, the bound alone decides.
A program may use at most 128 MiB of HBM per device.

v0:
```python
import math
import jax
import jax.numpy as jnp
from jax import lax
from jax.sharding import PartitionSpec as P


def tables(order_of, longitudes):
    longitude = jnp.arange(longitudes, dtype=jnp.int32)
    phases = order_of[:, None] * longitude[None, :] % longitudes
    angles = phases.astype(jnp.float32) * (2.0 * math.pi / longitudes)
    return jnp.stack([jnp.cos(angles), jnp.sin(angles)])


def sample_sums(product):
    return jnp.sum(product, axis=(0, 1, 3))


def shards(
    position, residual, direction, legendre, order_of, class_idx, land, class_weight, damping
):
    highest = lax.Precision.HIGHEST
    m_local = position.shape[0]
    samples = position.shape[2]
    deg_local = position.shape[3]
    band_rows = legendre.shape[2]
    lat_index = lax.axis_index("lat")
    order_index = lax.axis_index("order")
    my_orders = lax.dynamic_slice_in_dim(order_of, order_index * m_local, m_local)
    deg_start = lat_index * deg_local
    own_degrees = deg_start + jnp.arange(deg_local, dtype=jnp.int32)
    own_valid = (own_degrees[None, :] >= my_orders[:, None]).astype(jnp.float32)[:, None, None, :]
    pos_m = position * own_valid
    res_m = residual * own_valid
    dir_m = direction * own_valid
    norm_before = lax.psum(sample_sums(res_m * res_m), ("order", "lat"))
    block_part = lax.all_gather(direction, "lat", axis=3, tiled=True)
    degree_count = block_part.shape[3]
    in_block = jnp.arange(degree_count, dtype=jnp.int32)
    in_triangle = (in_block[None, :] >= my_orders[:, None]).astype(jnp.float32)
    masked = block_part * in_triangle[:, None, None, :]
    synthesis = jnp.einsum("mskd,mdt->mtsk", masked, legendre, precision=highest)
    grid_in = lax.all_to_all(
        synthesis.reshape(m_local, band_rows, 2 * samples),
        "order",
        split_axis=1,
        concat_axis=0,
        tiled=True,
    )
    orders_all = grid_in.shape[0]
    rows_here = grid_in.shape[1]
    grid_in = grid_in.reshape(orders_all, rows_here, 2, samples)
    longitudes = class_idx.shape[1]
    harmonic = tables(order_of, longitudes)
    surface = jnp.einsum("mrsk,sml->rkl", grid_in, harmonic, precision=highest)
    class_count = class_weight.shape[0]
    onehot = (
        class_idx[:, :, None] == jnp.arange(class_count, dtype=jnp.int32)[None, None, :]
    ).astype(jnp.float32)
    by_class = jnp.dot(onehot, class_weight, precision=highest)
    weight_grid = jnp.where(land == 1, by_class[:, :, 1], by_class[:, :, 0])
    weighted = surface * weight_grid[:, None, :]
    spectra = jnp.einsum("rkl,sml->mrsk", weighted, harmonic, precision=highest) * (
        2.0 / longitudes
    )
    returned = lax.all_to_all(
        spectra.reshape(orders_all, rows_here, 2 * samples),
        "order",
        split_axis=0,
        concat_axis=1,
        tiled=True,
    )
    returned = returned.reshape(m_local, band_rows, 2, samples)
    band_part = jnp.einsum("mtsk,mdt->mskd", returned, legendre, precision=highest)
    totals = lax.psum(band_part, "lat")
    summed = lax.dynamic_slice_in_dim(totals, deg_start, deg_local, 3)
    applied = (summed + damping[None, None, None, :] * dir_m) * own_valid
    curvature_sum = lax.psum(sample_sums(dir_m * applied), ("order", "lat"))
    step_size = (norm_before / curvature_sum)[None, None, :, None]
    new_residual = res_m - step_size * applied
    norm_after = lax.psum(sample_sums(new_residual * new_residual), ("order", "lat"))
    ratio_new = (norm_after / norm_before)[None, None, :, None]
    new_position = pos_m + step_size * dir_m
    new_direction = new_residual + ratio_new * dir_m
    return (new_position, new_residual, new_direction)


def solution(mesh):
    return jax.shard_map(
        shards,
        mesh=mesh,
        in_specs=(
            P("order", None, None, "lat"),
            P("order", None, None, "lat"),
            P("order", None, None, "lat"),
            P("order", None, "lat"),
            P(),
            P(("lat", "order"), None),
            P(("lat", "order"), None),
            P(),
            P("lat"),
        ),
        out_specs=(
            P("order", None, None, "lat"),
            P("order", None, None, "lat"),
            P("order", None, None, "lat"),
        ),
        check_vma=False,
    )
```

profile of v0, /device:TPU:1, one launch (start us, length us, event | category | flops | bytes accessed | tf_op | source)
XLA Modules:
  0.0 419.9 jit_solution(14200132624685688203)
XLA Ops:
  7.2 0.0 copy-start
  7.2 0.0 all-gather.2.cloned.1.call-start
  7.2 2.3 copy.20
  9.6 0.0 all-gather.2.cloned.1.call-update
  9.6 0.1 dynamic_slice.6
  9.7 0.7 fusion.11
  10.4 0.1 fusion.30
  10.6 0.9 fusion.37
  11.4 9.9 %fusion.17 = (f32[1,128,4320]{1,2,0:T(8,128)S(1)}, f32[1,128,4320]{1,2,0:T(8,128)}) fusion(s32[128]{0:T(128)S(1)} %copy-done.10), kind=kLoop, calls=%fused_computation.23 | loop fusion | flops 4976640 | bytes 4424192 | tf_op jit(solution)/shard_map/cos | solution.py:12
  21.3 44.9 %all-gather.2.cloned.1.call-done = f32[2,2,64,2160]{2,1,0,3:T(2,128)} async-done(((f32[2,2,64,540]{2,1,0,3:T(2,128)}), f32[2,2,64,2160]{2,1,0,3:T(2,128)}) %all-gather.2.cloned.1.call-update) | async-done | bytes 2211856 | tf_op jit(solution)/shard_map/all_gather | solution.py:37
  66.2 6.6 %broadcast_multiply_fusion = f32[2,2,64,2160]{2,1,0,3:T(2,128)S(1)} fusion(f32[2,2,64,2160]{2,1,0,3:T(2,128)} %all-gather.2.cloned.1.call-done, f32[2,2160]{0,1:T(8,128)S(1)} %fusion.30), kind=kLoop, calls=%fused_computation.18 | loop fusion | flops 552960 | bytes 4440960 | tf_op jit(solution)/shard_map/mul | solution.py:41
  72.8 8.7 %fusion.4 = f32[2,2,64,512]{3,2,1,0:T(8,128)S(1)} fusion(f32[2,2160,512]{2,1,0:T(8,128)S(1)} %copy-done.1, f32[2,2,64,2160]{2,1,0,3:T(2,128)S(1)} %broadcast_multiply_fusion), kind=kOutput, calls=%fused_computation.5 | convolution fusion | flops 3397386240 | bytes 11583488 | tf_op jit(solution)/shard_map/mskd,mdt->mtsk/dot_general | solution.py:42
  81.5 1.0 copy.22
  82.5 10.8 %all-to-all-start = ((f32[2,512,128]{2,0,1:T(2,128)}), f32[2,512,128]{2,0,1:T(2,128)S(1)}, u32[]{:S(2)}, u32[]{:S(2)}) async-start(f32[2,512,128]{2,0,1:T(2,128)} %copy.22), calls=%async_computation | async-start | bytes 1048576 | tf_op jit(solution)/shard_map/all_to_all | solution.py:43
  93.3 0.2 all-reduce.3.cloned.1.call-start
  93.6 17.4 %all-to-all-done = f32[2,512,128]{2,0,1:T(2,128)S(1)} async-done(((f32[2,512,128]{2,0,1:T(2,128)}), f32[2,512,128]{2,0,1:T(2,128)S(1)}, u32[]{:S(2)}, u32[]{:S(2)}) %all-to-all-start) | async-done | bytes 524320 | tf_op jit(solution)/shard_map/all_to_all | solution.py:43
  111.0 0.8 copy.24
  111.9 1.6 reshape.148
  113.5 31.3 %fusion.8 = f32[8,64,4320,1]{2,1,3,0:T(8,128)S(1)} fusion(f32[1,128,4320]{1,2,0:T(8,128)} %get-tuple-element.13, f32[1,128,4320]{1,2,0:T(8,128)S(1)} %get-tuple-element.12, f32[128,8,2,64]{3,2,1,0:T(2,128)S(1)} %reshape.148), kind=kOutput, calls=%fused_computation.10 | convolution fusion | flops 6795878400 | bytes 13795328 | tf_op jit(solution)/shard_map/mrsk,sml->rkl/dot_general | solution.py:55
  144.8 7.8 %fusion.24 = f32[128,8,2,64]{0,3,1,2:T(8,128)S(1)} fusion(f32[8,64,4320,1]{2,1,3,0:T(8,128)S(1)} %fusion.8, f32[8,4320]{1,0:T(8,128)S(1)} %fusion.33, f32[1,128,4320]{1,2,0:T(8,128)S(1)} %copy-done.2, f32[1,128,4320]{1,2,0:T(8,128)S(1)} %get-tuple-element.12), kind=kOutput, calls=%fused_computation.26 | convolution fusion | flops 6798221312 | bytes 13933568 | tf_op jit(solution)/shard_map/rkl,sml->mrsk/dot_general | solution.py:63
  152.7 0.2 copy.28
  153.0 23.3 %all_to_all.30 = f32[128,8,128]{2,1,0:T(8,128)S(1)} all-to-all(f32[128,8,128]{2,1,0:T(8,128)S(1)} %copy.28), channel_id=1, replica_groups=mesh['order'=64,'lat'=4] {'order'}, dimensions={0} | all-to-all | bytes 1048576 | tf_op jit(solution)/shard_map/all_to_all | solution.py:66
  176.3 0.6 reshape.150
  176.9 19.2 %fusion.2 = f32[2,2,64,2160]{3,2,1,0:T(8,128)} fusion(f32[2,2160,512]{2,1,0:T(8,128)} %param.12, f32[2,512,2,64]{3,2,1,0:T(2,128)S(1)} %reshape.150), kind=kOutput, calls=%fused_computation.3 | convolution fusion | flops 3397386240 | bytes 11583488 | tf_op jit(solution)/shard_map/mtsk,mdt->mskd/dot_general | solution.py:74
  196.2 0.0 all-reduce.3.cloned.1.call-update
  196.2 0.1 compare_convert_fusion
  196.3 61.3 %all-reduce.3.cloned.1.call-done = f32[2,2,64,2160]{3,2,1,0:T(8,128)} async-done(((f32[2,2,64,2160]{3,2,1,0:T(8,128)}), f32[2,2,64,2160]{3,2,1,0:T(8,128)}) %all-reduce.3.cloned.1.call-update) | async-done | bytes 2211856 | tf_op jit(solution)/shard_map/psum | solution.py:75
  257.6 1.6 multiply_reduce_fusion.1
  259.2 76.0 %all-reduce = (f32[64]{0:T(128)S(1)}, f32[64]{0:T(128)S(1)}) all-reduce(f32[64]{0:T(128)S(1)} %get-tuple-element.4, f32[64]{0:T(128)S(1)} %get-tuple-element.3), channel_id=1, replica_groups=mesh['order'=64,'lat'=4] {'order','lat'}, use_global_device_ids=true, to_apply=%region_1.0 | all-reduce | flops 128 | bytes 1024 | tf_op jit(solution)/shard_map/psum | solution.py:36
  335.1 2.5 multiply_reduce_fusion
  337.6 74.3 %psum.31 = f32[64]{0:T(128)S(1)} all-reduce(f32[64]{0:T(128)S(1)} %get-tuple-element.7), channel_id=1, replica_groups=mesh['order'=64,'lat'=4] {'order','lat'}, use_global_device_ids=true, to_apply=%region_6.7 | all-reduce | flops 64 | bytes 512 | tf_op jit(solution)/shard_map/psum | solution.py:81
  411.9 1.0 multiply_add_fusion
  (30 shorter events, 0.2 us)
Async XLA Ops:
  7.2 2.5 copy-start
  7.2 2.4 copy-start.10
  7.2 2.5 copy-start.11
  7.2 59.0 %all-gather.2.cloned.1.call-start = ((), (), s32[]{:S(2)}) async-start(), calls=%async_computation.2 | async-start | bytes 5529600 | tf_op jit(solution)/shard_map/all_gather | solution.py:37
  66.2 6.6 %copy-start.1 = (f32[2,2160,512]{2,1,0:T(8,128)S(1)}, f32[2,2160,512]{2,1,0:T(8,128)}, u32[]{:S(2)}) copy-start(f32[2,2160,512]{2,1,0:T(8,128)} %param.12) | copy-start | bytes 26542084
  72.7 20.8 %copy-start.7 = (f32[8,4320,1]{1,2,0:T(1,128)S(1)}, f32[8,4320,1]{1,2,0:T(1,128)}, u32[]{:S(2)}) copy-start(f32[8,4320,1]{1,2,0:T(1,128)} %get-tuple-element.11) | copy-start | bytes 414724
  72.8 20.8 %copy-start.8 = (s32[8,4320]{1,0:T(8,128)S(1)}, s32[8,4320]{1,0:T(8,128)}, u32[]{:S(2)}) copy-start(s32[8,4320]{1,0:T(8,128)} %param.15) | copy-start | bytes 414724
  82.5 28.5 %all-to-all-start = ((f32[2,512,128]{2,0,1:T(2,128)}), f32[2,512,128]{2,0,1:T(2,128)S(1)}, u32[]{:S(2)}, u32[]{:S(2)}) async-start(f32[2,512,128]{2,0,1:T(2,128)} %copy.22), calls=%async_computation | async-start | bytes 1048576 | tf_op jit(solution)/shard_map/all_to_all | solution.py:43
  93.3 164.3 %all-reduce.3.cloned.1.call-start = ((), (), s32[]{:S(2)}) async-start(), calls=%async_computation.3 | async-start | bytes 4456448 | tf_op jit(solution)/shard_map/psum | solution.py:75
  113.5 31.3 %copy-start.2 = (f32[1,128,4320]{1,2,0:T(8,128)S(1)}, f32[1,128,4320]{1,2,0:T(8,128)}, u32[]{:S(2)}) copy-start(f32[1,128,4320]{1,2,0:T(8,128)} %get-tuple-element.13) | copy-start | bytes 6635524
  196.2 61.4 %copy-start.3 = (f32[2,2,64,540]{3,2,1,0:T(8,128)S(1)}, f32[2,2,64,540]{3,2,1,0:T(8,128)}, u32[]{:S(2)}) copy-start(f32[2,2,64,540]{3,2,1,0:T(8,128)} %param.11) | copy-start | bytes 1658884
  196.2 61.4 %copy-start.4 = (f32[2,2,64,540]{3,2,1,0:T(8,128)S(1)}, f32[2,2,64,540]{3,2,1,0:T(8,128)}, u32[]{:S(2)}) copy-start(f32[2,2,64,540]{3,2,1,0:T(8,128)} %param.10) | copy-start | bytes 1658884
  196.2 61.4 %copy-start.9 = (f32[540]{0:T(1024)S(1)}, f32[540]{0:T(1024)}, u32[]{:S(2)}) copy-start(f32[540]{0:T(1024)} %param.17) | copy-start | bytes 6484
  196.2 138.9 %copy-start.6 = (f32[2,2,64,540]{3,2,1,0:T(8,128)S(1)}, f32[2,2,64,540]{3,2,1,0:T(8,128)}, u32[]{:S(2)}) copy-start(f32[2,2,64,540]{3,2,1,0:T(8,128)} %param.9) | copy-start | bytes 1658884
  337.6 75.3 %copy-start.5 = (f32[2,2,64,540]{3,2,1,0:T(8,128)}, f32[2,2,64,540]{3,2,1,0:T(8,128)S(1)}, u32[]{:S(2)}) copy-start(f32[2,2,64,540]{3,2,1,0:T(8,128)S(1)} %get-tuple-element.8) | copy-start | bytes 1658884
Sparse Core Ops, SparseCore 0:
  9.8 56.2 all-gather.1
  196.3 61.1 all-reduce.2
where the time goes:
time: 429 us; the launch traced here: 420 us
  blocking collectives  174 us (41%)
  waiting for transfers between devices  124 us (29%)
  matrix products  67.8 us (16%)
  other arithmetic  21.7 us (5%)
  between operations  14.5 us (3%)
  starting transfers between devices  11.1 us (3%)
  local copies, waits for them, and re-layouts  7.76 us (2%)
    psum x1, blocking collectives, shards(): norm_before = lax.psum(sample_sums(res_m * res_m), ('order', 'lat'))  76 us
    psum x1, blocking collectives, shards(): lax.psum(sample_sums(new_residual * new_residual), ('order', 'lat'))  74.3 us
    psum x1, waiting for transfers between devices, shards(): totals = lax.psum(band_part, 'lat')  61.3 us
    all_gather x1, waiting for transfers between devices, shards(): block_part = lax.all_gather(direction, 'lat', axis=3, tiled=True)  44.9 us
    dot_general x1, matrix products, shards(): surface = jnp.einsum('mrsk,sml->rkl', grid_in, harmonic, precision=highest)  31.3 us
    all_to_all x1, blocking collectives, shards(): lax.all_to_all(spectra.reshape(orders_all, rows_here, 2 * samples), 'orde...  23.3 us
    dot_general x1, matrix products, shards(): jnp.einsum('mtsk,mdt->mskd', returned, legendre, precision=highest)  19.2 us
    all_to_all x1, waiting for transfers between devices, shards(): lax.all_to_all(synthesis.reshape(m_local, band_rows, 2 * samples), 'order...  17.4 us
  transfers between devices with their start and end apart: 3, of which 3 were waited for; matrix products, arithmetic and copies ran while one was open for 3% of the time, Pallas kernels for 0%

commit v1 on v0

--- a/solution.py
+++ b/solution.py
@@ -40,13 +40,20 @@
     in_triangle = (in_block[None, :] >= my_orders[:, None]).astype(jnp.float32)
     masked = block_part * in_triangle[:, None, None, :]
     synthesis = jnp.einsum("mskd,mdt->mtsk", masked, legendre, precision=highest)
-    grid_in = lax.all_to_all(
-        synthesis.reshape(m_local, band_rows, 2 * samples),
-        "order",
-        split_axis=1,
-        concat_axis=0,
-        tiled=True,
-    )
+
+    def _keep_up_trails(raw, peer_axis):
+        p_next = jnp.concatenate(
+            lax.all_to_all(
+                jnp.stack(jnp.split(raw, lax.axis_size(peer_axis), axis=1)),
+                peer_axis,
+                split_axis=0,
+                concat_axis=0,
+            ),
+            axis=0,
+        )
+        return p_next
+
+    grid_in = _keep_up_trails(synthesis.reshape(m_local, band_rows, 2 * samples), "order")
     orders_all = grid_in.shape[0]
     rows_here = grid_in.shape[1]
     grid_in = grid_in.reshape(orders_all, rows_here, 2, samples)

time: 429 us -> 557 us (1.30)
  local copies, waits for them, and re-layouts: 7.76 us -> 139 us
    unnamed x25 -> x162, local copies, waits for them, and re-layouts: 2.38 us -> 129 us
    split x0 -> x4, local copies, waits for them, and re-layouts: none -> 6.47 us  [_keep_up_trails(): jnp.split(raw, lax.axis_size(peer_axis), axis=1)]
  transfers between devices with their start and end apart: 3 -> 3, of which waited for: 3 -> 3; matrix products, arithmetic and copies ran while one was open for 3% -> 2% of each run, Pallas kernels for 0% -> 0%
where the time goes in v1:
time: 557 us; the launch traced here: 552 us
  blocking collectives  174 us (31%)
  local copies, waits for them, and re-layouts  139 us (25%)
  waiting for transfers between devices  122 us (22%)
  matrix products  67.6 us (12%)
  other arithmetic  22.8 us (4%)
  between operations  14.8 us (3%)
  starting transfers between devices  11.6 us (2%)
    unnamed x162, local copies, waits for them, and re-layouts  129 us
    psum x1, blocking collectives, shards(): norm_before = lax.psum(sample_sums(res_m * res_m), ('order', 'lat'))  76 us
    psum x1, blocking collectives, shards(): lax.psum(sample_sums(new_residual * new_residual), ('order', 'lat'))  74.3 us
    psum x1, waiting for transfers between devices, shards(): totals = lax.psum(band_part, 'lat')  61.3 us
    all_gather x1, waiting for transfers between devices, shards(): block_part = lax.all_gather(direction, 'lat', axis=3, tiled=True)  44.9 us
    dot_general x1, matrix products, shards(): surface = jnp.einsum('mrsk,sml->rkl', grid_in, harmonic, precision=highest)  31 us
    all_to_all x1, blocking collectives, shards(): lax.all_to_all(spectra.reshape(orders_all, rows_here, 2 * samples), 'orde...  23.4 us
    dot_general x1, matrix products, shards(): jnp.einsum('mtsk,mdt->mskd', returned, legendre, precision=highest)  19.3 us
  transfers between devices with their start and end apart: 3, of which 3 were waited for; matrix products, arithmetic and copies ran while one was open for 2% of the time, Pallas kernels for 0%

profile of v1, /device:TPU:1, one launch (start us, length us, event | category | flops | bytes accessed | tf_op | source)
XLA Modules:
  0.0 552.0 jit_solution(15473635999809441217)
XLA Ops:
  7.2 2.3 copy.90
  11.4 9.8 %fusion.17 = (f32[1,128,4320]{1,2,0:T(8,128)S(1)}, f32[1,128,4320]{1,2,0:T(8,128)}) fusion(s32[128]{0:T(128)S(1)} %copy-done.15), kind=kLoop, calls=%fused_computation.23 | loop fusion | flops 4976640 | bytes 4424192 | tf_op jit(solution)/shard_map/cos | solution.py:12
  21.3 44.9 %all-gather.2.cloned.1.call-done = f32[2,2,64,2160]{2,1,0,3:T(2,128)} async-done(((f32[2,2,64,540]{2,1,0,3:T(2,128)}), f32[2,2,64,2160]{2,1,0,3:T(2,128)}) %all-gather.2.cloned.1.call-update) | async-done | bytes 2211856 | tf_op jit(solution)/shard_map/all_gather | solution.py:37
  66.2 6.8 %broadcast_multiply_fusion = f32[2,2,64,2160]{2,1,0,3:T(2,128)S(1)} fusion(f32[2,2,64,2160]{2,1,0,3:T(2,128)} %all-gather.2.cloned.1.call-done, f32[2,2160]{0,1:T(8,128)S(1)} %fusion.30), kind=kLoop, calls=%fused_computation.18 | loop fusion | flops 552960 | bytes 4440960 | tf_op jit(solution)/shard_map/mul | solution.py:41
  73.0 8.7 %fusion.4 = f32[2,2,64,512]{3,2,1,0:T(8,128)S(1)} fusion(f32[2,2160,512]{2,1,0:T(8,128)S(1)} %copy-done.1, f32[2,2,64,2160]{2,1,0,3:T(2,128)S(1)} %broadcast_multiply_fusion), kind=kOutput, calls=%fused_computation.5 | convolution fusion | flops 3397386240 | bytes 11583488 | tf_op jit(solution)/shard_map/mskd,mdt->mtsk/dot_general | solution.py:42
  82.0 2.0 fusion.39
  84.0 2.1 fusion.38
  86.1 2.1 fusion.37
  92.8 1.6 copy.173
  100.6 1.6 copy.178
  103.8 1.6 copy.180
  107.0 1.6 copy.182
  110.1 1.6 copy.184
  117.9 1.6 copy.189
  121.0 1.6 copy.191
  122.6 1.6 copy.192
  124.2 1.6 copy.193
  125.8 1.6 copy.194
  127.4 1.6 copy.195
  129.0 1.6 copy.196
  215.1 11.0 %all-to-all-start = ((f32[64,2,8,128]{3,2,1,0:T(8,128)}), f32[64,2,8,128]{3,2,1,0:T(8,128)}, u32[]{:S(2)}, u32[]{:S(2)}) async-start(f32[64,2,8,128]{3,2,1,0:T(8,128)} %constant_dynamic-update-slice_fusion), calls=%async_computation | async-start | bytes 1048576 | tf_op jit(solution)/shard_map/all_to_all | solution.py:46
  227.6 16.1 %all-to-all-done = f32[64,2,8,128]{3,2,1,0:T(8,128)} async-done(((f32[64,2,8,128]{3,2,1,0:T(8,128)}), f32[64,2,8,128]{3,2,1,0:T(8,128)}, u32[]{:S(2)}, u32[]{:S(2)}) %all-to-all-start) | async-done | bytes 524320 | tf_op jit(solution)/shard_map/all_to_all | solution.py:46
  243.8 1.6 reshape_reshape.3
  245.4 31.0 %fusion.8 = f32[8,64,4320,1]{2,1,3,0:T(8,128)S(1)} fusion(f32[1,128,4320]{1,2,0:T(8,128)} %get-tuple-element.77, f32[1,128,4320]{1,2,0:T(8,128)S(1)} %get-tuple-element.76, f32[128,8,2,64]{3,2,1,0:T(2,128)S(1)} %reshape_reshape.3), kind=kOutput, calls=%fused_computation.10 | convolution fusion | flops 6795878400 | bytes 13795328 | tf_op jit(solution)/shard_map/mrsk,sml->rkl/dot_general | solution.py:62
  276.5 7.8 %fusion.24 = f32[128,8,2,64]{0,3,1,2:T(8,128)S(1)} fusion(f32[8,64,4320,1]{2,1,3,0:T(8,128)S(1)} %fusion.8, f32[8,4320]{1,0:T(8,128)S(1)} %fusion.33, f32[1,128,4320]{1,2,0:T(8,128)S(1)} %copy-done.2, f32[1,128,4320]{1,2,0:T(8,128)S(1)} %get-tuple-element.76), kind=kOutput, calls=%fused_computation.26 | convolution fusion | flops 6798221312 | bytes 13933568 | tf_op jit(solution)/shard_map/rkl,sml->mrsk/dot_general | solution.py:70
  284.6 23.4 %all_to_all.20 = f32[128,8,128]{2,1,0:T(8,128)S(1)} all-to-all(f32[128,8,128]{2,1,0:T(8,128)S(1)} %copy.159), channel_id=1, replica_groups=mesh['order'=64,'lat'=4] {'order'}, dimensions={0} | all-to-all | bytes 1048576 | tf_op jit(solution)/shard_map/all_to_all | solution.py:73
  308.7 19.3 %fusion.2 = f32[2,2,64,2160]{3,2,1,0:T(8,128)} fusion(f32[2,2160,512]{2,1,0:T(8,128)} %param.12, f32[2,512,2,64]{3,2,1,0:T(2,128)S(1)} %reshape.145), kind=kOutput, calls=%fused_computation.3 | convolution fusion | flops 3397386240 | bytes 11583488 | tf_op jit(solution)/shard_map/mtsk,mdt->mskd/dot_general | solution.py:81
  328.1 61.3 %all-reduce.3.cloned.1.call-done = f32[2,2,64,2160]{3,2,1,0:T(8,128)} async-done(((f32[2,2,64,2160]{3,2,1,0:T(8,128)}), f32[2,2,64,2160]{3,2,1,0:T(8,128)}) %all-reduce.3.cloned.1.call-update) | async-done | bytes 2211856 | tf_op jit(solution)/shard_map/psum | solution.py:82
  389.4 1.6 multiply_reduce_fusion.1
  391.0 76.0 %all-reduce = (f32[64]{0:T(128)S(1)}, f32[64]{0:T(128)S(1)}) all-reduce(f32[64]{0:T(128)S(1)} %get-tuple-element.4, f32[64]{0:T(128)S(1)} %get-tuple-element.3), channel_id=1, replica_groups=mesh['order'=64,'lat'=4] {'order','lat'}, use_global_device_ids=true, to_apply=%region_1.0 | all-reduce | flops 128 | bytes 1024 | tf_op jit(solution)/shard_map/psum | solution.py:36
  466.9 2.5 multiply_reduce_fusion
  469.4 74.3 %psum.31 = f32[64]{0:T(128)S(1)} all-reduce(f32[64]{0:T(128)S(1)} %get-tuple-element.7), channel_id=1, replica_groups=mesh['order'=64,'lat'=4] {'order','lat'}, use_global_device_ids=true, to_apply=%region_6.7 | all-reduce | flops 64 | bytes 512 | tf_op jit(solution)/shard_map/psum | solution.py:88
  (169 shorter events, 113.5 us)
Async XLA Ops:
  7.2 2.5 copy-start
  7.2 2.4 copy-start.15
  7.2 2.5 copy-start.16
  7.2 59.0 %all-gather.2.cloned.1.call-start = ((), (), s32[]{:S(2)}) async-start(), calls=%async_computation.2 | async-start | bytes 5529600 | tf_op jit(solution)/shard_map/all_gather | solution.py:37
  66.2 6.8 %copy-start.1 = (f32[2,2160,512]{2,1,0:T(8,128)S(1)}, f32[2,2160,512]{2,1,0:T(8,128)}, u32[]{:S(2)}) copy-start(f32[2,2160,512]{2,1,0:T(8,128)} %param.12) | copy-start | bytes 26542084
  103.8 41.5 %copy-start.13 = (f32[2,8,128]{1,2,0:T(8,128)S(1)}, f32[2,8,128]{1,2,0:T(8,128)}, u32[]{:S(2)}) copy-start(f32[2,8,128]{1,2,0:T(8,128)} %get-tuple-element.27) | copy-start | bytes 24580
  122.6 33.4 %copy-start.12 = (f32[2,8,128]{1,2,0:T(8,128)S(1)}, f32[2,8,128]{1,2,0:T(8,128)}, u32[]{:S(2)}) copy-start(f32[2,8,128]{1,2,0:T(8,128)} %get-tuple-element.15) | copy-start | bytes 24580
  124.2 31.9 %copy-start.11 = (f32[2,8,128]{1,2,0:T(8,128)S(1)}, f32[2,8,128]{1,2,0:T(8,128)}, u32[]{:S(2)}) copy-start(f32[2,8,128]{1,2,0:T(8,128)} %get-tuple-element.14) | copy-start | bytes 24580
  125.8 30.4 %copy-start.10 = (f32[2,8,128]{1,2,0:T(8,128)S(1)}, f32[2,8,128]{1,2,0:T(8,128)}, u32[]{:S(2)}) copy-start(f32[2,8,128]{1,2,0:T(8,128)} %get-tuple-element.13) | copy-start | bytes 24580
  127.4 28.8 %copy-start.9 = (f32[2,8,128]{1,2,0:T(8,128)S(1)}, f32[2,8,128]{1,2,0:T(8,128)}, u32[]{:S(2)}) copy-start(f32[2,8,128]{1,2,0:T(8,128)} %get-tuple-element.12) | copy-start | bytes 24580
  129.0 27.3 %copy-start.8 = (f32[2,8,128]{1,2,0:T(8,128)S(1)}, f32[2,8,128]{1,2,0:T(8,128)}, u32[]{:S(2)}) copy-start(f32[2,8,128]{1,2,0:T(8,128)} %get-tuple-element.11) | copy-start | bytes 24580
  145.3 81.4 %copy-start.7 = (f32[8,4320,1]{1,2,0:T(1,128)S(1)}, f32[8,4320,1]{1,2,0:T(1,128)}, u32[]{:S(2)}) copy-start(f32[8,4320,1]{1,2,0:T(1,128)} %get-tuple-element.75) | copy-start | bytes 414724
  215.1 28.6 %all-to-all-start = ((f32[64,2,8,128]{3,2,1,0:T(8,128)}), f32[64,2,8,128]{3,2,1,0:T(8,128)}, u32[]{:S(2)}, u32[]{:S(2)}) async-start(f32[64,2,8,128]{3,2,1,0:T(8,128)} %constant_dynamic-update-slice_fusion), calls=%async_computation | async-start | bytes 1048576 | tf_op jit(solution)/shard_map/all_to_all | solution.py:46
  226.2 163.2 %all-reduce.3.cloned.1.call-start = ((), (), s32[]{:S(2)}) async-start(), calls=%async_computation.3 | async-start | bytes 4456448 | tf_op jit(solution)/shard_map/psum | solution.py:82
  245.4 31.1 %copy-start.2 = (f32[1,128,4320]{1,2,0:T(8,128)S(1)}, f32[1,128,4320]{1,2,0:T(8,128)}, u32[]{:S(2)}) copy-start(f32[1,128,4320]{1,2,0:T(8,128)} %get-tuple-element.77) | copy-start | bytes 6635524
  328.0 61.4 %copy-start.3 = (f32[2,2,64,540]{3,2,1,0:T(8,128)S(1)}, f32[2,2,64,540]{3,2,1,0:T(8,128)}, u32[]{:S(2)}) copy-start(f32[2,2,64,540]{3,2,1,0:T(8,128)} %param.11) | copy-start | bytes 1658884
  328.0 61.4 %copy-start.4 = (f32[2,2,64,540]{3,2,1,0:T(8,128)S(1)}, f32[2,2,64,540]{3,2,1,0:T(8,128)}, u32[]{:S(2)}) copy-start(f32[2,2,64,540]{3,2,1,0:T(8,128)} %param.10) | copy-start | bytes 1658884
  328.0 61.4 %copy-start.14 = (f32[540]{0:T(1024)S(1)}, f32[540]{0:T(1024)}, u32[]{:S(2)}) copy-start(f32[540]{0:T(1024)} %param.17) | copy-start | bytes 6484
  328.0 138.9 %copy-start.6 = (f32[2,2,64,540]{3,2,1,0:T(8,128)S(1)}, f32[2,2,64,540]{3,2,1,0:T(8,128)}, u32[]{:S(2)}) copy-start(f32[2,2,64,540]{3,2,1,0:T(8,128)} %param.9) | copy-start | bytes 1658884
  469.4 75.3 %copy-start.5 = (f32[2,2,64,540]{3,2,1,0:T(8,128)}, f32[2,2,64,540]{3,2,1,0:T(8,128)S(1)}, u32[]{:S(2)}) copy-start(f32[2,2,64,540]{3,2,1,0:T(8,128)S(1)} %get-tuple-element.8) | copy-start | bytes 1658884
Sparse Core Ops, SparseCore 0:
  9.8 56.2 all-gather.1
  328.1 61.1 all-reduce.2
